TPU v7x, 32 devices: a whole 2x2x4 slice. The times are simulated.
32 devices in a mesh: ctx: 8 (over z, x), head: 4 (over y, core).
Axes of the slice: x: 2, y: 2, z: 4, core: 2. Of those that a mesh axis runs over, the one named last changes fastest.
Arguments:
- q_nope: bfloat16 [1024, 4096], P('ctx', 'head'), may hold values from -6 to 6
- q_rope: bfloat16 [1024, 2048], P('ctx', 'head'), may hold values from -300 to 300
- latent: bfloat16 [1024, 512], P('ctx'), may hold values from -6 to 6
- k_rope: bfloat16 [1024, 64], P('ctx'), may hold values from -4 to 4
- span_order: int32 [16], replicated, may hold values from 0 to 15, each once
- w_uk: bfloat16 [512, 4096], P(None, 'head'), may hold values from -0.25 to 0.25
- w_uv: bfloat16 [512, 4096], P(None, 'head'), may hold values from -0.25 to 0.25
- w_o: bfloat16 [4096, 7168], P('head', 'ctx'), may hold values from -0.125 to 0.125
Outputs:
- attended: bfloat16 [1024, 7168], P('ctx', 'head')
Inputs may be any that keep to these rules, and one draw needn't show every extreme that they name: `span_order`: a permutation of 0 to 15.
All inputs are finite; a program needn't handle non-finite values.
Results may differ from a plain program's by a relative error of at most 0.014.
Values may be sent and summed in bfloat16 or wider, within the bound.
No kernel may reach another device: no remote copies, remote signals or barrier semaphores. Data moves between devices by JAX's collectives and lax.ppermute only.
A program may use at most 128 MiB of HBM per device.

v0:
```python
import math
import jax
import jax.numpy as jnp
from jax import lax
from jax.sharding import PartitionSpec as P

LAT = 512
ROPE = 64
NOPE = 128
VDIM = 128


def span_place(slot_ids, table):
    match = slot_ids[:, None] == jnp.arange(table.shape[0], dtype=jnp.int32)[None, :]
    return jnp.sum(jnp.where(match, table[None, :], 0), axis=1)


def local(q_nope, q_rope, latent, k_rope, span_order, w_uk, w_uv, w_o):
    rows = q_nope.shape[0]
    half = rows // 2
    heads = w_uk.shape[1] // NOPE
    scale = 1.0 / math.sqrt(NOPE + ROPE)
    local_rows = jnp.arange(rows, dtype=jnp.int32)
    query_slot = lax.axis_index("ctx") * 2 + local_rows // half
    qpos = span_place(query_slot, span_order) * half + local_rows % half
    absorbed = jnp.einsum(
        "thn,lhn->htl",
        q_nope.reshape(rows, heads, NOPE),
        w_uk.reshape(LAT, heads, NOPE),
        preferred_element_type=jnp.float32,
    ).astype(jnp.bfloat16)
    rotary = q_rope.reshape(rows, heads, ROPE)
    lat_piece = lax.all_gather(latent, "ctx", axis=0, tiled=True)
    rope_piece = lax.all_gather(k_rope, "ctx", axis=0, tiled=True)
    count = lat_piece.shape[0]
    key_rows = jnp.arange(count, dtype=jnp.int32)
    kpos = span_place(key_rows // half, span_order) * half + key_rows % half
    running = jnp.full((heads, rows), -1e30, jnp.float32)
    score = jnp.einsum("htl,kl->htk", absorbed, lat_piece, preferred_element_type=jnp.float32)
    score = score + jnp.einsum(
        "thr,kr->htk", rotary, rope_piece, preferred_element_type=jnp.float32
    )
    score = score * scale
    visible = kpos[None, None, :] <= qpos[None, :, None]
    newest = jnp.maximum(running, jnp.max(jnp.where(visible, score, -1e30), axis=-1))
    weight = jnp.where(visible, jnp.exp(score - newest[..., None]), 0.0)
    summed = jnp.sum(weight, axis=-1)
    accum = jnp.einsum(
        "htk,kl->htl", weight.astype(jnp.bfloat16), lat_piece, preferred_element_type=jnp.float32
    )
    running, summed, accum = (newest, summed, accum)
    context = (accum / summed[..., None]).astype(jnp.bfloat16)
    heads_out = jnp.einsum(
        "htl,lhv->thv", context, w_uv.reshape(LAT, heads, VDIM), preferred_element_type=jnp.float32
    ).astype(jnp.bfloat16)
    heads_out = heads_out.reshape(rows, heads * VDIM)
    every_token = jnp.dot(
        lax.all_gather(heads_out, "ctx", axis=0, tiled=True),
        w_o,
        preferred_element_type=jnp.float32,
    ).astype(jnp.bfloat16)
    partial_value = lax.all_to_all(every_token, "ctx", split_axis=0, concat_axis=1, tiled=True)
    return (
        lax.psum_scatter(partial_value, "head", scatter_dimension=1, tiled=True)
        .astype(jnp.float32)
        .astype(jnp.bfloat16)
    )


def solution(mesh):
    placed = (
        P("ctx", "head"),
        P("ctx", "head"),
        P("ctx", None),
        P("ctx", None),
        P(),
        P(None, "head"),
        P(None, "head"),
        P("head", "ctx"),
    )
    return jax.shard_map(
        local, mesh=mesh, in_specs=placed, out_specs=P("ctx", "head"), check_vma=False
    )
```

profile of v0, /device:TPU:0, one launch (start us, length us, event | category | flops | bytes accessed | tf_op | source)
XLA Modules:
  0.0 204.4 jit_solution(16470658505095125386)
XLA Ops:
  6.5 0.0 copy-start
  6.5 0.0 all-gather.3.cloned.1.call-start
  6.5 0.7 all-gather.3.cloned.1.call-update
  7.3 0.0 all-gather.5.cloned.1.call-start
  7.3 1.0 copy.19
  8.3 2.3 %copy.24 = bf16[512,1024]{0,1:T(8,128)(2,1)} copy(bf16[512,1024]{1,0:T(8,128)(2,1)} %param.14) | data formatting | bytes 2097152 | tf_op jit(solution)/shard_map/reshape | solution.py:54
  10.6 28.3 %all_gather.10 = bf16[1024,64]{0,1:T(8,128)(2,1)S(1)} all-gather(bf16[128,64]{0,1:T(8,128)(2,1)} %param.11), channel_id=1, replica_groups=mesh['ctx'=8,'head'=4] {'ctx'}, dimensions={0}, use_global_device_ids=true | all-gather | bytes 147456 | tf_op jit(solution)/shard_map/all_gather | solution.py:34
  39.0 0.7 select_reduce_fusion.2
  39.7 0.7 select_reduce_fusion.1
  40.5 0.1 broadcast_compare_fusion
  40.6 12.1 %all-gather.3.cloned.1.call-done = bf16[1024,512]{1,0:T(8,128)(2,1)} async-done(((bf16[128,512]{1,0:T(8,128)(2,1)}), bf16[1024,512]{1,0:T(8,128)(2,1)}) %all-gather.3.cloned.1.call-update) | async-done | bytes 1048592 | tf_op jit(solution)/shard_map/all_gather | solution.py:33
  52.8 5.1 %fusion.8 = f32[8,128,1024]{2,1,0:T(8,128)} fusion(bf16[1024,512]{1,0:T(8,128)(2,1)} %all-gather.3.cloned.1.call-done, bf16[512,1024]{1,0:T(8,128)(2,1)} %param.13, bf16[128,1024]{1,0:T(8,128)(2,1)} %param.8), kind=kOutput, calls=%fused_computation.13 | convolution fusion | flops 1208483840 | bytes 6553600 | tf_op jit(solution)/shard_map/htl,kl->htk/dot_general | solution.py:39
  57.9 3.3 %select_reduce_fusion = (f32[8,128]{1,0:T(8,128)S(1)}, f32[8,128,1024]{2,1,0:T(8,128)S(1)}) fusion(pred[128,1024]{1,0:T(8,128)(4,1)S(1)} %broadcast_compare_fusion, f32[8,128,1024]{2,1,0:T(8,128)} %fusion.8, bf16[128,8,64]{0,2,1:T(8,128)(2,1)S(1)} %bitcast.53, bf16[1024,64]{0,1:T(8,128)(2,1)S(1)} %all_gather.10), kind=kOutput, calls=%fused_computation.3 | convolution fusion | flops 138411008 | bytes 8785920 | tf_op jit(solution)/shard_map/thr,kr->htk/dot_general | solution.py:40
  61.2 0.0 copy-start.1
  61.2 0.0 copy-start.2
  61.2 1.9 copy-done.1
  63.1 1.1 fusion.1
  64.3 0.0 copy-done.2
  64.3 4.8 %convolution_convert_fusion.2 = bf16[8,128,128]{1,2,0:T(8,128)(2,1)} fusion(bf16[512,8,128]{0,2,1:T(8,128)(2,1)} %bitcast.52, f32[8,128]{1,0:T(8,128)S(1)} %fusion.1, f32[8,128,1024]{2,1,0:T(8,128)} %copy-done.1, f32[8,128]{1,0:T(8,128)S(1)} %broadcast_maximum_fusion, pred[128,1024]{1,0:T(8,128)(4,1)S(1)} %broadcast_compare_fusion, ...), kind=kOutput, calls=%fused_computation.14 | convolution fusion | flops 1212284928 | bytes 6692864 | tf_op jit(solution)/shard_map/htl,lhv->thv/dot_general | solution.py:53
  69.1 0.0 all-gather.5.cloned.1.call-update
  69.1 0.0 reduce-scatter.2.cloned.1.call-start
  69.1 49.2 %all-gather.5.cloned.1.call-done = bf16[1024,1024]{0,1:T(8,128)(2,1)} async-done(((bf16[128,1024]{0,1:T(8,128)(2,1)}), bf16[1024,1024]{0,1:T(8,128)(2,1)}) %all-gather.5.cloned.1.call-update) | async-done | bytes 2097168 | tf_op jit(solution)/shard_map/all_gather | solution.py:58
  118.3 0.0 copy-done
  118.3 4.0 %convolution_convert_fusion = bf16[1024,896]{1,0:T(8,128)(2,1)S(1)} fusion(bf16[1024,1024]{0,1:T(8,128)(2,1)} %all-gather.5.cloned.1.call-done, bf16[1024,896]{1,0:T(8,128)(2,1)S(1)} %copy-done), kind=kOutput, calls=%fused_computation.11 | convolution fusion | flops 1879965696 | bytes 5767168 | tf_op jit(solution)/shard_map/dot_general | solution.py:57
  122.3 45.3 %all_to_all.19 = bf16[8,128,896]{2,1,0:T(8,128)(2,1)S(1)} all-to-all(bf16[8,128,896]{2,1,0:T(8,128)(2,1)S(1)} %bitcast.51), channel_id=1, replica_groups=mesh['ctx'=8,'head'=4] {'ctx'}, dimensions={0} | all-to-all | bytes 3670016 | tf_op jit(solution)/shard_map/all_to_all | solution.py:62
  167.5 1.5 copy.27
  169.1 0.0 reduce-scatter.2.cloned.1.call-update
  169.1 28.8 %reduce-scatter.2.cloned.1.call-done = bf16[128,1792]{1,0:T(8,128)(2,1)} async-done(((bf16[128,7168]{1,0:T(8,128)(2,1)}), bf16[128,1792]{1,0:T(8,128)(2,1)}) %reduce-scatter.2.cloned.1.call-update) | async-done | bytes 458768 | tf_op jit(solution)/shard_map/reduce_scatter | solution.py:64
  (5 shorter events, 0.0 us)
Async XLA Ops:
  6.5 111.8 %copy-start = (bf16[1024,896]{1,0:T(8,128)(2,1)S(1)}, bf16[1024,896]{1,0:T(8,128)(2,1)}, u32[]{:S(2)}) copy-start(bf16[1024,896]{1,0:T(8,128)(2,1)} %param.15) | copy-start | bytes 5505028
  6.5 46.2 %all-gather.3.cloned.1.call-start = ((), (), s32[]{:S(2)}) async-start(), calls=%async_computation.2 | async-start | bytes 1179648 | tf_op jit(solution)/shard_map/all_gather | solution.py:33
  7.3 111.0 %all-gather.5.cloned.1.call-start = ((), (), s32[]{:S(2)}) async-start(), calls=%async_computation.3 | async-start | bytes 2359296 | tf_op jit(solution)/shard_map/all_gather | solution.py:58
  61.2 1.9 copy-start.1
  61.2 3.0 %copy-start.2 = (bf16[1024,512]{1,0:T(8,128)(2,1)S(1)}, bf16[1024,512]{1,0:T(8,128)(2,1)}, u32[]{:S(2)}) copy-start(bf16[1024,512]{1,0:T(8,128)(2,1)} %all-gather.3.cloned.1.call-done) | copy-start | bytes 3145732
  69.1 128.8 %reduce-scatter.2.cloned.1.call-start = ((), (), s32[]{:S(2)}) async-start(), calls=%async_computation.4 | async-start | bytes 2293760 | tf_op jit(solution)/shard_map/reduce_scatter | solution.py:64
Sparse Core Ops, SparseCore 0:
  9.5 43.2 all-gather.2
  69.2 49.0 all-gather.4
  169.2 28.5 reduce-scatter.1
where the time goes:
time: 205 us; the launch traced here: 204 us
  waiting for transfers between devices  90.8 us (44%)
  blocking collectives  73.6 us (36%)
  matrix products  17.2 us (8%)
  between operations  13.2 us (6%)
  local copies, waits for them, and re-layouts  6.76 us (3%)
  other arithmetic  2.76 us (1%)
    all_gather x1, waiting for transfers between devices, local(): lax.all_gather(heads_out, 'ctx', axis=0, tiled=True)  49.2 us
    all_to_all x1, blocking collectives, local(): lax.all_to_all(every_token, 'ctx', split_axis=0, concat_axis=1, tiled=True)  45.3 us
    reduce_scatter x1, waiting for transfers between devices, local(): lax.psum_scatter(partial_value, 'head', scatter_dimension=1, tiled=True)  28.8 us
    all_gather x1, blocking collectives, local(): rope_piece = lax.all_gather(k_rope, 'ctx', axis=0, tiled=True)  28.3 us
    all_gather x1, waiting for transfers between devices, local(): lat_piece = lax.all_gather(latent, 'ctx', axis=0, tiled=True)  12.1 us
    dot_general x1, matrix products, local(): jnp.einsum('htl,kl->htk', absorbed, lat_piece, preferred_element_type=jnp...  5.13 us
    dot_general x1, matrix products, local(): jnp.einsum('htl,lhv->thv', context, w_uv.reshape(LAT, heads, VDIM), prefe...  4.77 us
  transfers between devices with their start and end apart: 3, of which 3 were waited for; matrix products, arithmetic and copies ran while one was open for 2% of the time, Pallas kernels for 0%

commit v1 on v0

--- a/solution.py
+++ b/solution.py
@@ -1,3 +1,4 @@
+import functools
 import math
 import jax
 import jax.numpy as jnp
@@ -8,6 +9,21 @@
 ROPE = 64
 NOPE = 128
 VDIM = 128
+
+
+def detail_marks(array_here, axis_name):
+    return jnp.concatenate(
+        lax.all_to_all(
+            jnp.stack(jnp.split(array_here, lax.psum(1, axis_name=axis_name), axis=0), axis=0),
+            axis_name=axis_name,
+            split_axis=0,
+            concat_axis=0,
+        ),
+        axis=1,
+    )
+
+
+tables_spread = functools.partial(detail_marks, axis_name="ctx")
 
 
 def span_place(slot_ids, table):
@@ -59,7 +75,7 @@
         w_o,
         preferred_element_type=jnp.float32,
     ).astype(jnp.bfloat16)
-    partial_value = lax.all_to_all(every_token, "ctx", split_axis=0, concat_axis=1, tiled=True)
+    partial_value = tables_spread(every_token)
     return (
         lax.psum_scatter(partial_value, "head", scatter_dimension=1, tiled=True)
         .astype(jnp.float32)

time: 205 us -> 208 us (1.015)
  local copies, waits for them, and re-layouts: 6.76 us -> 10.2 us
    reshape x0 -> x1, local copies, waits for them, and re-layouts: none -> 3.77 us  [detail_marks(): jnp.concatenate(lax.all_to_all(jnp.stack(jnp.split(array_here, lax.psum(1...]
where the time goes in v1:
time: 208 us
  waiting for transfers between devices  92.6 us (45%)
  blocking collectives  73.6 us (35%)
  matrix products  16.8 us (8%)
  between operations  13.3 us (6%)
  local copies, waits for them, and re-layouts  10.2 us (5%)
    all_gather x1, waiting for transfers between devices, local(): lax.all_gather(heads_out, 'ctx', axis=0, tiled=True)  49.2 us
    all_to_all x1, blocking collectives, detail_marks(): lax.all_to_all(jnp.stack(jnp.split(array_here, lax.psum(1, axis_name=axis...  45.5 us
    reduce_scatter x1, waiting for transfers between devices, local(): lax.psum_scatter(partial_value, 'head', scatter_dimension=1, tiled=True)  28.7 us
    all_gather x1, blocking collectives, local(): rope_piece = lax.all_gather(k_rope, 'ctx', axis=0, tiled=True)  28.1 us
    all_gather x1, waiting for transfers between devices, local(): lat_piece = lax.all_gather(latent, 'ctx', axis=0, tiled=True)  14 us
    dot_general x1, matrix products, local(): jnp.einsum('htl,lhv->thv', context, w_uv.reshape(LAT, heads, VDIM), prefe...  4.77 us
    dot_general x1, matrix products, local(): jnp.einsum('htl,kl->htk', absorbed, lat_piece, preferred_element_type=jnp...  4.76 us
  transfers between devices with their start and end apart: 3, of which 3 were waited for; matrix products, arithmetic and copies ran while one was open for 2% of the time, Pallas kernels for 0%

profile of v1, /device:TPU:0, one launch (start us, length us, event | category | flops | bytes accessed | tf_op | source)
XLA Modules:
  0.0 208.0 jit_solution(6260573859067052583)
XLA Ops:
  6.5 0.0 copy-start
  6.5 0.0 copy-start.5
  6.5 0.0 copy-start.6
  6.5 0.0 copy-start.2
  6.5 0.0 copy-start.4
  6.5 0.0 all-gather.3.cloned.1.call-start
  6.6 0.7 all-gather.3.cloned.1.call-update
  7.3 0.0 all-gather.5.cloned.1.call-start
  7.3 1.0 copy.19
  8.4 2.3 %copy.25 = bf16[512,1024]{0,1:T(8,128)(2,1)} copy(bf16[512,1024]{1,0:T(8,128)(2,1)} %param.14) | data formatting | bytes 2097152 | tf_op jit(solution)/shard_map/reshape | solution.py:70
  10.6 0.0 copy-done.5
  10.7 28.1 %all_gather.10 = bf16[1024,64]{0,1:T(8,128)(2,1)S(1)} all-gather(bf16[128,64]{0,1:T(8,128)(2,1)S(1)} %copy-done.5), channel_id=1, replica_groups=mesh['ctx'=8,'head'=4] {'ctx'}, dimensions={0}, use_global_device_ids=true | all-gather | bytes 147456 | tf_op jit(solution)/shard_map/all_gather | solution.py:50
  38.8 0.0 copy-done.6
  38.8 0.1 select_reduce_fusion.2
  38.9 0.1 select_reduce_fusion.1
  39.0 0.1 broadcast_compare_fusion
  39.1 14.0 %all-gather.3.cloned.1.call-done = bf16[1024,512]{1,0:T(8,128)(2,1)} async-done(((bf16[128,512]{1,0:T(8,128)(2,1)}), bf16[1024,512]{1,0:T(8,128)(2,1)}) %all-gather.3.cloned.1.call-update) | async-done | bytes 1048592 | tf_op jit(solution)/shard_map/all_gather | solution.py:49
  53.2 0.0 copy-done.2
  53.2 0.0 copy-done.4
  53.2 4.8 %fusion.8 = f32[8,128,1024]{2,1,0:T(8,128)} fusion(bf16[1024,512]{1,0:T(8,128)(2,1)} %all-gather.3.cloned.1.call-done, bf16[512,1024]{1,0:T(8,128)(2,1)S(1)} %copy-done.2, bf16[128,1024]{1,0:T(8,128)(2,1)S(1)} %copy-done.4), kind=kOutput, calls=%fused_computation.13 | convolution fusion | flops 1208483840 | bytes 6553600 | tf_op jit(solution)/shard_map/htl,kl->htk/dot_general | solution.py:55
  57.9 3.3 %select_reduce_fusion = (f32[8,128]{1,0:T(8,128)S(1)}, f32[8,128,1024]{2,1,0:T(8,128)S(1)}) fusion(pred[128,1024]{1,0:T(8,128)(4,1)S(1)} %broadcast_compare_fusion, f32[8,128,1024]{2,1,0:T(8,128)} %fusion.8, bf16[128,8,64]{0,2,1:T(8,128)(2,1)S(1)} %bitcast.82, bf16[1024,64]{0,1:T(8,128)(2,1)S(1)} %all_gather.10), kind=kOutput, calls=%fused_computation.3 | convolution fusion | flops 138411008 | bytes 8785920 | tf_op jit(solution)/shard_map/thr,kr->htk/dot_general | solution.py:56
  61.3 0.0 copy-start.1
  61.3 0.0 copy-start.3
  61.3 1.1 fusion.1
  62.4 0.8 copy-done.1
  63.2 0.1 copy-done.3
  63.3 4.8 %convolution_convert_fusion.2 = bf16[8,128,128]{1,2,0:T(8,128)(2,1)} fusion(bf16[512,8,128]{0,2,1:T(8,128)(2,1)} %bitcast.81, f32[8,128]{1,0:T(8,128)S(1)} %fusion.1, f32[8,128,1024]{2,1,0:T(8,128)} %copy-done.1, f32[8,128]{1,0:T(8,128)S(1)} %broadcast_maximum_fusion, pred[128,1024]{1,0:T(8,128)(4,1)S(1)} %broadcast_compare_fusion, ...), kind=kOutput, calls=%fused_computation.14 | convolution fusion | flops 1212284928 | bytes 6692864 | tf_op jit(solution)/shard_map/htl,lhv->thv/dot_general | solution.py:69
  68.1 0.0 all-gather.5.cloned.1.call-update
  68.1 0.0 reduce-scatter.2.cloned.1.call-start
  68.1 49.2 %all-gather.5.cloned.1.call-done = bf16[1024,1024]{0,1:T(8,128)(2,1)} async-done(((bf16[128,1024]{0,1:T(8,128)(2,1)}), bf16[1024,1024]{0,1:T(8,128)(2,1)}) %all-gather.5.cloned.1.call-update) | async-done | bytes 2097168 | tf_op jit(solution)/shard_map/all_gather | solution.py:74
  117.3 0.0 copy-done
  117.3 4.0 %convolution_convert_fusion = bf16[1024,896]{1,0:T(8,128)(2,1)S(1)} fusion(bf16[1024,1024]{0,1:T(8,128)(2,1)} %all-gather.5.cloned.1.call-done, bf16[1024,896]{1,0:T(8,128)(2,1)S(1)} %copy-done), kind=kOutput, calls=%fused_computation.11 | convolution fusion | flops 1879965696 | bytes 5767168 | tf_op jit(solution)/shard_map/dot_general | solution.py:73
  121.6 45.5 %all_to_all.5 = bf16[8,128,896]{2,1,0:T(8,128)(2,1)} all-to-all(bf16[8,128,896]{2,1,0:T(8,128)(2,1)S(1)} %fusion.27), channel_id=1, replica_groups=mesh['ctx'=8,'head'=4] {'ctx'}, dimensions={0} | all-to-all | bytes 3670016 | tf_op jit(solution)/shard_map/all_to_all | solution.py:16
  167.0 3.8 %copy.22 = bf16[128,8,896]{0,2,1:T(8,128)(2,1)} copy(bf16[128,8,896]{2,0,1:T(8,128)(2,1)} %bitcast.80) | data formatting | bytes 3670016 | tf_op jit(solution)/shard_map/reshape | solution.py:15
  170.8 0.0 reduce-scatter.2.cloned.1.call-update
  170.8 28.7 %reduce-scatter.2.cloned.1.call-done = bf16[128,1792]{0,1:T(8,128)(2,1)} async-done(((bf16[128,7168]{0,1:T(8,128)(2,1)}), bf16[128,1792]{0,1:T(8,128)(2,1)}) %reduce-scatter.2.cloned.1.call-update) | async-done | bytes 458768 | tf_op jit(solution)/shard_map/reduce_scatter | solution.py:80
  199.5 2.0 copy.23
  (13 shorter events, 0.2 us)
Async XLA Ops:
  6.5 110.8 %copy-start = (bf16[1024,896]{1,0:T(8,128)(2,1)S(1)}, bf16[1024,896]{1,0:T(8,128)(2,1)}, u32[]{:S(2)}) copy-start(bf16[1024,896]{1,0:T(8,128)(2,1)} %param.15) | copy-start | bytes 5505028
  6.5 4.1 %copy-start.5 = (bf16[128,64]{0,1:T(8,128)(2,1)S(1)}, bf16[128,64]{0,1:T(8,128)(2,1)}, u32[]{:S(2)}) copy-start(bf16[128,64]{0,1:T(8,128)(2,1)} %param.11) | copy-start | bytes 49156
  6.5 32.2 %copy-start.6 = (s32[16]{0:T(128)S(1)}, s32[16]{0:T(128)}, u32[]{:S(2)}) copy-start(s32[16]{0:T(128)} %param.12) | copy-start | bytes 196
  6.5 46.6 %copy-start.2 = (bf16[512,1024]{1,0:T(8,128)(2,1)S(1)}, bf16[512,1024]{1,0:T(8,128)(2,1)}, u32[]{:S(2)}) copy-start(bf16[512,1024]{1,0:T(8,128)(2,1)} %param.13) | copy-start | bytes 3145732
  6.5 46.6 %copy-start.4 = (bf16[128,1024]{1,0:T(8,128)(2,1)S(1)}, bf16[128,1024]{1,0:T(8,128)(2,1)}, u32[]{:S(2)}) copy-start(bf16[128,1024]{1,0:T(8,128)(2,1)} %param.8) | copy-start | bytes 786436
  6.5 46.6 %all-gather.3.cloned.1.call-start = ((), (), s32[]{:S(2)}) async-start(), calls=%async_computation.2 | async-start | bytes 1179648 | tf_op jit(solution)/shard_map/all_gather | solution.py:49
  7.3 110.0 %all-gather.5.cloned.1.call-start = ((), (), s32[]{:S(2)}) async-start(), calls=%async_computation.3 | async-start | bytes 2359296 | tf_op jit(solution)/shard_map/all_gather | solution.py:74
  61.3 1.9 copy-start.1
  61.3 2.0 copy-start.3
  68.1 131.4 %reduce-scatter.2.cloned.1.call-start = ((), (), s32[]{:S(2)}) async-start(), calls=%async_computation.4 | async-start | bytes 2293760 | tf_op jit(solution)/shard_map/reduce_scatter | solution.py:80
Sparse Core Ops, SparseCore 0:
  9.5 43.6 all-gather.2
  68.2 49.0 all-gather.4
  170.9 28.4 reduce-scatter.1
